TPU v7x, 512 devices: a whole 4x4x16 slice. The times are simulated.
512 devices in a mesh: seq: 64 (over z, y), dp: 8 (over x, core).
Axes of the slice: x: 4, y: 4, z: 16, core: 2. Of those that a mesh axis runs over, the one named last changes fastest.
Arguments:
- queries: bfloat16 [8, 8192, 2048], P('dp', 'seq'), may hold values from -40 to 40
- keys: bfloat16 [8, 8192, 2048], P('dp', 'seq'), may hold values from -6 to 6
- values: bfloat16 [8, 8192, 2048], P('dp', 'seq'), may hold values from -6 to 6
- grad_out: bfloat16 [8, 8192, 2048], P('dp', 'seq'), may hold values from -48 to 48
- lengths: int32 [8], P('dp'), may hold values from 1024 to 8192, as said below
- fields: int32 [8, 8192], P('dp', 'seq'), may hold values from 0 to 63
- field_bias: bfloat16 [16, 64], replicated, may hold values from -6 to 6
Outputs:
- grad_queries: bfloat16 [8, 8192, 2048], P('dp', 'seq')
- grad_keys: bfloat16 [8, 8192, 2048], P('dp', 'seq')
- grad_values: bfloat16 [8, 8192, 2048], P('dp', 'seq')
- grad_bias: float32 [16, 64], replicated
Inputs may be any that keep to these rules, and one draw needn't show every extreme that they name: `lengths`: the valid positions of a sequence form a prefix; in every draw some sequence is full.
All inputs are finite; a program needn't handle non-finite values.
Results may differ from a plain program's by a relative error of at most 0.0077.
Values may be sent and summed in bfloat16 or wider, within the bound.
A program may use at most 128 MiB of HBM per device.

v0:
```python
import jax
import jax.numpy as jnp
from jax import lax
from jax.sharding import PartitionSpec as P

HEADS = 16
HEAD_DIM = 128
WINDOW = 512
FIELDS = 64


def passed_along(value, axis, steps):
    count = lax.axis_size(axis)
    first, last = (max(0, -steps), min(count, count - steps))
    return lax.ppermute(value, axis, [(source, source + steps) for source in range(first, last)])


def split_heads(rows):
    return rows.reshape(rows.shape[0], HEADS, HEAD_DIM)


def band_mask(query_places, key_places, length):
    not_after = key_places[None, :] <= query_places[:, None]
    inside = key_places[None, :] > query_places[:, None] - WINDOW
    started = key_places[None, :] >= 0
    live_rows = query_places[:, None] < length
    return not_after & inside & started & live_rows


def logits_of(query_heads, key_heads, key_bias):
    factor = HEAD_DIM ** (-0.5)
    products = jnp.einsum(
        "qhd,khd->hqk", query_heads, key_heads, preferred_element_type=jnp.float32
    )
    return products * factor + key_bias[:, None, :]


def grad_logits_of(attn_weights, row_delta, grad_heads, value_heads):
    grad_probs = jnp.einsum(
        "qhd,khd->hqk", grad_heads, value_heads, preferred_element_type=jnp.float32
    )
    return attn_weights * (grad_probs - row_delta[:, :, None])


def shards(queries, keys, values, grad_out, lengths, fields, field_bias):
    tok_rows = queries.shape[1]
    row_width = queries.shape[2]
    length = lengths[0]
    query_own = queries[0]
    key_own = keys[0]
    value_own = values[0]
    grad_own = grad_out[0]
    reach_blocks = WINDOW // tok_rows
    factor = HEAD_DIM ** (-0.5)
    block_index = lax.axis_index("seq")
    onehot = (fields[0][:, None] == jnp.arange(FIELDS, dtype=jnp.int32)[None, :]).astype(
        jnp.bfloat16
    )
    own_bias = jnp.dot(field_bias, onehot.T, preferred_element_type=jnp.float32).astype(
        jnp.bfloat16
    )
    package = (key_own, value_own, own_bias)
    arrived = []
    for distance in range(1, reach_blocks + 1):
        arrived.append(passed_along((package[0], package[1], package[2]), "seq", distance))
    ordered = arrived[::-1] + [package]
    key_all = jnp.concatenate([arrival[0] for arrival in ordered], axis=0)
    value_all = jnp.concatenate([arrival[1] for arrival in ordered], axis=0)
    bias_all = jnp.concatenate([arrival[2] for arrival in ordered], axis=1).astype(jnp.float32)
    query_places = block_index * tok_rows + jnp.arange(tok_rows, dtype=jnp.int32)
    key_places = (block_index - reach_blocks) * tok_rows + jnp.arange(
        (reach_blocks + 1) * tok_rows, dtype=jnp.int32
    )
    query_heads = split_heads(query_own)
    grad_heads = split_heads(grad_own)
    key_heads = split_heads(key_all)
    value_heads = split_heads(value_all)
    logits = logits_of(query_heads, key_heads, bias_all)
    visible = band_mask(query_places, key_places, length)[None]
    live_rows = (query_places < length)[None, :, None]
    row_peak = jnp.max(jnp.where(visible, logits, -1e30), axis=2, keepdims=True)
    powers = jnp.where(visible, jnp.exp(logits - row_peak), 0.0)
    totals = jnp.where(live_rows, jnp.sum(powers, axis=2, keepdims=True), 1.0)
    attn_weights = powers / totals
    weights_low = attn_weights.astype(jnp.bfloat16)
    outputs = jnp.einsum(
        "hqk,khd->qhd", weights_low, value_heads, preferred_element_type=jnp.float32
    )
    row_delta = jnp.einsum("qhd,qhd->hq", grad_heads.astype(jnp.float32), outputs)
    grad_logits = grad_logits_of(attn_weights, row_delta, grad_heads, value_heads)
    grad_low = grad_logits.astype(jnp.bfloat16)
    grad_query = (
        jnp.einsum("hqk,khd->qhd", grad_low, key_heads, preferred_element_type=jnp.float32) * factor
    )
    own_cols = reach_blocks * tok_rows
    grad_key = (
        jnp.einsum(
            "hqk,qhd->khd", grad_low, query_heads, preferred_element_type=jnp.float32
        ).reshape(-1, row_width)
        * factor
    )
    grad_value = jnp.einsum(
        "hqk,qhd->khd", weights_low, grad_heads, preferred_element_type=jnp.float32
    ).reshape(-1, row_width)
    column = jnp.sum(grad_logits, axis=1)
    key_total = grad_key[own_cols:]
    value_total = grad_value[own_cols:]
    column_total = column[:, own_cols:]
    for distance in range(1, reach_blocks + 1):
        first_row = (reach_blocks - distance) * tok_rows
        returned = passed_along(
            (
                grad_key[first_row : first_row + tok_rows],
                grad_value[first_row : first_row + tok_rows],
                column[:, first_row : first_row + tok_rows],
            ),
            "seq",
            -distance,
        )
        key_total = key_total + returned[0]
        value_total = value_total + returned[1]
        column_total = column_total + returned[2]
    bias_local = jnp.dot(column_total, onehot.astype(jnp.float32), precision=lax.Precision.HIGHEST)
    query_low = grad_query.reshape(tok_rows, row_width).astype(jnp.bfloat16)
    key_low = key_total.astype(jnp.bfloat16)
    value_low = value_total.astype(jnp.bfloat16)
    bias_total = lax.psum(bias_local, ("seq", "dp"))
    return (
        query_low.reshape(1, tok_rows, row_width),
        key_low.reshape(1, tok_rows, row_width),
        value_low.reshape(1, tok_rows, row_width),
        bias_total,
    )


def solution(mesh):
    return jax.shard_map(
        shards,
        mesh=mesh,
        in_specs=(
            P("dp", "seq", None),
            P("dp", "seq", None),
            P("dp", "seq", None),
            P("dp", "seq", None),
            P("dp"),
            P("dp", "seq"),
            P(),
        ),
        out_specs=(P("dp", "seq", None), P("dp", "seq", None), P("dp", "seq", None), P()),
        check_vma=False,
    )
```

profile of v0, /device:TPU:1, one launch (start us, length us, event | category | flops | bytes accessed | tf_op | source)
XLA Modules:
  0.0 491.5 jit_solution(1476968906301964713)
XLA Ops:
  2.2 4.2 collective-permute-start.7
  6.4 4.5 collective-permute-start.6
  12.2 2.6 collective-permute-start.11
  14.9 4.8 collective-permute-start.10
  19.7 4.2 collective-permute-start.9
  24.6 2.6 collective-permute-start.5
  27.3 4.8 collective-permute-start.4
  38.1 5.2 %collective-permute-done.5 = bf16[16,128]{1,0:T(8,128)(2,1)S(1)} collective-permute-done((bf16[16,128]{1,0:T(8,128)(2,1)S(1)}, bf16[16,128]{1,0:T(8,128)(2,1)S(1)}, u32[]{:S(2)}, u32[]{:S(2)}) %collective-permute-start.5) | collective-permute-done | bytes 4128 | tf_op jit(solution)/shard_map/ppermute | solution.py:15
  44.7 18.3 %collective-permute-start.3 = (bf16[128,2048]{0,1:T(8,128)(2,1)S(1)}, bf16[128,2048]{0,1:T(8,128)(2,1)}, u32[]{:S(2)}, u32[]{:S(2)}) collective-permute-start(bf16[128,2048]{0,1:T(8,128)(2,1)S(1)} %bitcast.102), channel_id=1, source_target_pairs={{0,8},{8,16},{16,24},{24,32},{32,40},{40,48},{48,56},{56,64},{64,7... | collective-permute-start | bytes 1572872 | tf_op jit(solution)/shard_map/ppermute | solution.py:15
  63.0 9.7 %collective-permute-start.2 = (bf16[128,2048]{0,1:T(8,128)(2,1)S(1)}, bf16[128,2048]{0,1:T(8,128)(2,1)}, u32[]{:S(2)}, u32[]{:S(2)}) collective-permute-start(bf16[128,2048]{0,1:T(8,128)(2,1)S(1)} %bitcast.103), channel_id=1, source_target_pairs={{0,16},{8,24},{16,32},{24,40},{32,48},{40,56},{48,64},{56,72},{64,... | collective-permute-start | bytes 1572872 | tf_op jit(solution)/shard_map/ppermute | solution.py:15
  72.7 5.3 %collective-permute-start.1 = (bf16[128,2048]{0,1:T(8,128)(2,1)S(1)}, bf16[128,2048]{0,1:T(8,128)(2,1)}, u32[]{:S(2)}, u32[]{:S(2)}) collective-permute-start(bf16[128,2048]{0,1:T(8,128)(2,1)S(1)} %bitcast.104), channel_id=1, source_target_pairs={{0,24},{8,32},{16,40},{24,48},{32,56},{40,64},{48,72},{56,80},{64,... | collective-permute-start | bytes 1572872 | tf_op jit(solution)/shard_map/ppermute | solution.py:15
  78.0 2.1 collective-permute-start
  82.3 2.0 copy.38
  89.5 4.0 collective-permute-done.1
  104.6 7.6 %fusion.34 = (f32[16,128]{1,0:T(8,128)S(1)}, f32[16,128,640]{1,2,0:T(8,128)}) fusion(f32[16,640]{1,0:T(8,128)S(1)} %convert_element_type.46, pred[128,640]{0,1:T(8,128)(4,1)S(1)} %and_and_fusion, bf16[640,16,128]{2,0,1:T(8,128)(2,1)} %constant_dynamic-update-slice_fusion, bf16[128,16,128]{0,2,1:T(8,128)(2,1)} %bitcast.94), kind=kOutput, calls=%fused_computation.67 | convolution fusion | flops 681575040 | bytes 8519680 | tf_op jit(solution)/shard_map/sub | solution.py:82
  117.3 3.3 fusion.8
  122.6 2.6 copy.69
  126.9 5.2 %fusion.35 = (f32[16,640]{1,0:T(8,128)S(1)}, bf16[16,128,640]{1,2,0:T(8,128)(2,1)S(1)}) fusion(f32[16,128]{1,0:T(8,128)S(1)} %copy.70, bf16[640,16,128]{2,0,1:T(8,128)(2,1)} %copy-done.5, bf16[128,16,128]{0,2,1:T(8,128)(2,1)} %copy.55, f32[16,128,640]{1,2,0:T(8,128)} %get-tuple-element.27, f32[16,128]{1,0:T(8,128)S(1)} %broadcast_select_fusion), kind=kOutput, calls=%fused_computation.68 | convolution fusion | flops 342087680 | bytes 11067392 | tf_op jit(solution)/shard_map/qhd,khd->hqk/dot_general | solution.py:39
  133.5 2.4 fusion.32
  135.9 2.5 copy.52
  138.4 2.5 copy.51
  141.0 2.6 copy.50
  150.1 2.6 copy.53
  152.6 15.2 %collective-permute-done.20 = f32[16,128]{1,0:T(8,128)S(1)} collective-permute-done((f32[16,128]{1,0:T(8,128)S(1)}, f32[16,128]{1,0:T(8,128)S(1)}, u32[]{:S(2)}, u32[]{:S(2)}) %collective-permute-start.20) | collective-permute-done | bytes 8224 | tf_op jit(solution)/shard_map/ppermute | solution.py:15
  169.2 109.7 %collective-permute-done.23 = f32[16,128]{1,0:T(8,128)S(1)} collective-permute-done((f32[16,128]{1,0:T(8,128)S(1)}, f32[16,128]{1,0:T(8,128)S(1)}, u32[]{:S(2)}, u32[]{:S(2)}) %collective-permute-start.23) | collective-permute-done | bytes 8224 | tf_op jit(solution)/shard_map/ppermute | solution.py:15
  281.2 2.8 collective-permute-done.22
  290.2 2.7 copy.59
  292.9 2.6 copy.58
  300.7 2.8 fusion.11
  306.6 178.1 %psum.7 = f32[16,64]{1,0:T(8,128)} all-reduce(f32[16,64]{1,0:T(8,128)S(1)} %fusion.22), channel_id=1, replica_groups=mesh['seq'=64,'dp'=8] {'seq','dp'}, use_global_device_ids=true, to_apply=%region_3.4 | all-reduce | flops 1024 | bytes 8192 | tf_op jit(solution)/shard_map/psum | solution.py:127
  484.7 2.4 fusion.18
  488.1 3.4 fusion.19
  (113 shorter events, 64.3 us)
Async XLA Ops:
  0.6 35.0 %copy-start.12 = (bf16[1,128,2048]{2,1,0:T(8,128)(2,1)S(1)}, bf16[1,128,2048]{2,1,0:T(8,128)(2,1)}, u32[]{:S(2)}) copy-start(bf16[1,128,2048]{2,1,0:T(8,128)(2,1)} %param.7) | copy-start | bytes 1572868
  2.2 34.5 %copy-start.13 = (bf16[1,128,2048]{2,1,0:T(8,128)(2,1)S(1)}, bf16[1,128,2048]{2,1,0:T(8,128)(2,1)}, u32[]{:S(2)}) copy-start(bf16[1,128,2048]{2,1,0:T(8,128)(2,1)} %param.10) | copy-start | bytes 1572868
  2.2 22.4 %collective-permute-start.7 = (bf16[16,128]{1,0:T(8,128)(2,1)S(1)}, bf16[16,128]{1,0:T(8,128)(2,1)S(1)}, u32[]{:S(2)}, u32[]{:S(2)}) collective-permute-start(bf16[16,128]{1,0:T(8,128)(2,1)S(1)} %fusion.14), channel_id=1, source_target_pairs={{0,8},{8,16},{16,24},{24,32},{32,40},{40,48},{48,56},{56,64},{64,7... | collective-permute-start | bytes 12296 | tf_op jit(solution)/shard_map/ppermute | solution.py:15
  6.4 20.9 %collective-permute-start.6 = (bf16[16,128]{1,0:T(8,128)(2,1)S(1)}, bf16[16,128]{1,0:T(8,128)(2,1)S(1)}, u32[]{:S(2)}, u32[]{:S(2)}) collective-permute-start(bf16[16,128]{1,0:T(8,128)(2,1)S(1)} %fusion.14), channel_id=1, source_target_pairs={{0,16},{8,24},{16,32},{24,40},{32,48},{40,56},{48,64},{56,72},{64,... | collective-permute-start | bytes 12296 | tf_op jit(solution)/shard_map/ppermute | solution.py:15
  12.2 50.8 %collective-permute-start.11 = (bf16[128,2048]{0,1:T(8,128)(2,1)S(1)}, bf16[128,2048]{0,1:T(8,128)(2,1)S(1)}, u32[]{:S(2)}, u32[]{:S(2)}) collective-permute-start(bf16[128,2048]{0,1:T(8,128)(2,1)S(1)} %bitcast.96), channel_id=1, source_target_pairs={{0,8},{8,16},{16,24},{24,32},{32,40},{40,48},{48,56},{56,64},{64,7... | collective-permute-start | bytes 1572872 | tf_op jit(solution)/shard_map/ppermute | solution.py:15
  14.9 57.8 %collective-permute-start.10 = (bf16[128,2048]{0,1:T(8,128)(2,1)S(1)}, bf16[128,2048]{0,1:T(8,128)(2,1)S(1)}, u32[]{:S(2)}, u32[]{:S(2)}) collective-permute-start(bf16[128,2048]{0,1:T(8,128)(2,1)S(1)} %bitcast.97), channel_id=1, source_target_pairs={{0,16},{8,24},{16,32},{24,40},{32,48},{40,56},{48,64},{56,72},{64,... | collective-permute-start | bytes 1572872 | tf_op jit(solution)/shard_map/ppermute | solution.py:15
  19.7 58.3 %collective-permute-start.9 = (bf16[128,2048]{0,1:T(8,128)(2,1)S(1)}, bf16[128,2048]{0,1:T(8,128)(2,1)}, u32[]{:S(2)}, u32[]{:S(2)}) collective-permute-start(bf16[128,2048]{0,1:T(8,128)(2,1)S(1)} %bitcast.98), channel_id=1, source_target_pairs={{0,24},{8,32},{16,40},{24,48},{32,56},{40,64},{48,72},{56,80},{64,... | collective-permute-start | bytes 1572872 | tf_op jit(solution)/shard_map/ppermute | solution.py:15
  24.6 18.7 %collective-permute-start.5 = (bf16[16,128]{1,0:T(8,128)(2,1)S(1)}, bf16[16,128]{1,0:T(8,128)(2,1)S(1)}, u32[]{:S(2)}, u32[]{:S(2)}) collective-permute-start(bf16[16,128]{1,0:T(8,128)(2,1)S(1)} %fusion.14), channel_id=1, source_target_pairs={{0,24},{8,32},{16,40},{24,48},{32,56},{40,64},{48,72},{56,80},{64,... | collective-permute-start | bytes 12296 | tf_op jit(solution)/shard_map/ppermute | solution.py:15
  27.3 17.4 %collective-permute-start.4 = (bf16[16,128]{1,0:T(8,128)(2,1)S(1)}, bf16[16,128]{1,0:T(8,128)(2,1)S(1)}, u32[]{:S(2)}, u32[]{:S(2)}) collective-permute-start(bf16[16,128]{1,0:T(8,128)(2,1)S(1)} %fusion.14), channel_id=1, source_target_pairs={{0,32},{8,40},{16,48},{24,56},{32,64},{40,72},{48,80},{56,88},{64,... | collective-permute-start | bytes 12296 | tf_op jit(solution)/shard_map/ppermute | solution.py:15
  43.3 41.0 %collective-permute-start.8 = (bf16[128,2048]{0,1:T(8,128)(2,1)S(1)}, bf16[128,2048]{0,1:T(8,128)(2,1)S(1)}, u32[]{:S(2)}, u32[]{:S(2)}) collective-permute-start(bf16[128,2048]{0,1:T(8,128)(2,1)S(1)} %bitcast.100), channel_id=1, source_target_pairs={{0,32},{8,40},{16,48},{24,56},{32,64},{40,72},{48,80},{56,88},{64,... | collective-permute-start | bytes 1572872 | tf_op jit(solution)/shard_map/ppermute | solution.py:15
  44.7 40.7 %collective-permute-start.3 = (bf16[128,2048]{0,1:T(8,128)(2,1)S(1)}, bf16[128,2048]{0,1:T(8,128)(2,1)}, u32[]{:S(2)}, u32[]{:S(2)}) collective-permute-start(bf16[128,2048]{0,1:T(8,128)(2,1)S(1)} %bitcast.102), channel_id=1, source_target_pairs={{0,8},{8,16},{16,24},{24,32},{32,40},{40,48},{48,56},{56,64},{64,7... | collective-permute-start | bytes 1572872 | tf_op jit(solution)/shard_map/ppermute | solution.py:15
  63.0 24.4 %collective-permute-start.2 = (bf16[128,2048]{0,1:T(8,128)(2,1)S(1)}, bf16[128,2048]{0,1:T(8,128)(2,1)}, u32[]{:S(2)}, u32[]{:S(2)}) collective-permute-start(bf16[128,2048]{0,1:T(8,128)(2,1)S(1)} %bitcast.103), channel_id=1, source_target_pairs={{0,16},{8,24},{16,32},{24,40},{32,48},{40,56},{48,64},{56,72},{64,... | collective-permute-start | bytes 1572872 | tf_op jit(solution)/shard_map/ppermute | solution.py:15
  72.7 20.8 %collective-permute-start.1 = (bf16[128,2048]{0,1:T(8,128)(2,1)S(1)}, bf16[128,2048]{0,1:T(8,128)(2,1)}, u32[]{:S(2)}, u32[]{:S(2)}) collective-permute-start(bf16[128,2048]{0,1:T(8,128)(2,1)S(1)} %bitcast.104), channel_id=1, source_target_pairs={{0,24},{8,32},{16,40},{24,48},{32,56},{40,64},{48,72},{56,80},{64,... | collective-permute-start | bytes 1572872 | tf_op jit(solution)/shard_map/ppermute | solution.py:15
  78.0 17.5 %collective-permute-start = (bf16[128,2048]{0,1:T(8,128)(2,1)S(1)}, bf16[128,2048]{0,1:T(8,128)(2,1)}, u32[]{:S(2)}, u32[]{:S(2)}) collective-permute-start(bf16[128,2048]{0,1:T(8,128)(2,1)S(1)} %bitcast.105), channel_id=1, source_target_pairs={{0,32},{8,40},{16,48},{24,56},{32,64},{40,72},{48,80},{56,88},{64,... | collective-permute-start | bytes 1572872 | tf_op jit(solution)/shard_map/ppermute | solution.py:15
  96.9 6.0 %copy-start.11 = (bf16[128,16,128]{2,0,1:T(8,128)(2,1)S(1)}, bf16[128,16,128]{2,0,1:T(8,128)(2,1)}, u32[]{:S(2)}) copy-start(bf16[128,16,128]{2,0,1:T(8,128)(2,1)} %copy.32) | copy-start | bytes 1572868
  96.9 6.9 %copy-start.10 = (bf16[128,16,128]{2,0,1:T(8,128)(2,1)S(1)}, bf16[128,16,128]{2,0,1:T(8,128)(2,1)}, u32[]{:S(2)}) copy-start(bf16[128,16,128]{2,0,1:T(8,128)(2,1)} %copy.33) | copy-start | bytes 1572868
  126.9 5.2 %copy-start.8 = (bf16[1,128,2048]{1,2,0:T(8,128)(2,1)S(1)}, bf16[1,128,2048]{1,2,0:T(8,128)(2,1)}, u32[]{:S(2)}) copy-start(bf16[1,128,2048]{1,2,0:T(8,128)(2,1)} %copy.76) | copy-start | bytes 1572868
  141.0 139.2 %copy-start.7 = (bf16[128,16,128]{0,2,1:T(8,128)(2,1)S(1)}, bf16[128,16,128]{0,2,1:T(8,128)(2,1)}, u32[]{:S(2)}) copy-start(bf16[128,16,128]{0,2,1:T(8,128)(2,1)} %copy.55) | copy-start | bytes 1572868
  143.6 153.2 %collective-permute-start.12 = (f32[128,2048]{0,1:T(8,128)}, f32[128,2048]{0,1:T(8,128)}, u32[]{:S(2)}, u32[]{:S(2)}) collective-permute-start(f32[128,2048]{0,1:T(8,128)} %bitcast.111), channel_id=1, source_target_pairs={{8,0},{16,8},{24,16},{32,24},{40,32},{48,40},{56,48},{64,56},{72,6... | collective-permute-start | bytes 3145736 | tf_op jit(solution)/shard_map/ppermute | solution.py:15
  144.8 153.2 %collective-permute-start.13 = (f32[128,2048]{0,1:T(8,128)}, f32[128,2048]{0,1:T(8,128)}, u32[]{:S(2)}, u32[]{:S(2)}) collective-permute-start(f32[128,2048]{0,1:T(8,128)} %bitcast.110), channel_id=1, source_target_pairs={{16,0},{24,8},{32,16},{40,24},{48,32},{56,40},{64,48},{72,56},{80,... | collective-permute-start | bytes 3145736 | tf_op jit(solution)/shard_map/ppermute | solution.py:15
  146.1 153.2 %collective-permute-start.14 = (f32[128,2048]{0,1:T(8,128)}, f32[128,2048]{0,1:T(8,128)}, u32[]{:S(2)}, u32[]{:S(2)}) collective-permute-start(f32[128,2048]{0,1:T(8,128)} %bitcast.108), channel_id=1, source_target_pairs={{24,0},{32,8},{40,16},{48,24},{56,32},{64,40},{72,48},{80,56},{88,... | collective-permute-start | bytes 3145736 | tf_op jit(solution)/shard_map/ppermute | solution.py:15
  147.5 20.4 %collective-permute-start.20 = (f32[16,128]{1,0:T(8,128)S(1)}, f32[16,128]{1,0:T(8,128)S(1)}, u32[]{:S(2)}, u32[]{:S(2)}) collective-permute-start(f32[16,128]{1,0:T(8,128)S(1)} %get-tuple-element.22), channel_id=1, source_target_pairs={{8,0},{16,8},{24,16},{32,24},{40,32},{48,40},{56,48},{64,56},{72,6... | collective-permute-start | bytes 24584 | tf_op jit(solution)/shard_map/ppermute | solution.py:15
  148.8 130.1 %collective-permute-start.23 = (f32[16,128]{1,0:T(8,128)S(1)}, f32[16,128]{1,0:T(8,128)S(1)}, u32[]{:S(2)}, u32[]{:S(2)}) collective-permute-start(f32[16,128]{1,0:T(8,128)S(1)} %get-tuple-element.23), channel_id=1, source_target_pairs={{32,0},{40,8},{48,16},{56,24},{64,32},{72,40},{80,48},{88,56},{96,... | collective-permute-start | bytes 24584 | tf_op jit(solution)/shard_map/ppermute | solution.py:15
  167.9 116.2 %collective-permute-start.22 = (f32[16,128]{1,0:T(8,128)S(1)}, f32[16,128]{1,0:T(8,128)S(1)}, u32[]{:S(2)}, u32[]{:S(2)}) collective-permute-start(f32[16,128]{1,0:T(8,128)S(1)} %get-tuple-element.24), channel_id=1, source_target_pairs={{24,0},{32,8},{40,16},{48,24},{56,32},{64,40},{72,48},{80,56},{88,... | collective-permute-start | bytes 24584 | tf_op jit(solution)/shard_map/ppermute | solution.py:15
  278.9 205.8 %collective-permute-start.15 = (f32[128,2048]{0,1:T(8,128)}, f32[128,2048]{0,1:T(8,128)}, u32[]{:S(2)}, u32[]{:S(2)}) collective-permute-start(f32[128,2048]{0,1:T(8,128)} %bitcast.109), channel_id=1, source_target_pairs={{32,0},{40,8},{48,16},{56,24},{64,32},{72,40},{80,48},{88,56},{96,... | collective-permute-start | bytes 3145736 | tf_op jit(solution)/shard_map/ppermute | solution.py:15
  284.0 11.4 %collective-permute-start.21 = (f32[16,128]{1,0:T(8,128)S(1)}, f32[16,128]{1,0:T(8,128)S(1)}, u32[]{:S(2)}, u32[]{:S(2)}) collective-permute-start(f32[16,128]{1,0:T(8,128)S(1)} %get-tuple-element.25), channel_id=1, source_target_pairs={{16,0},{24,8},{32,16},{40,24},{48,32},{56,40},{64,48},{72,56},{80,... | collective-permute-start | bytes 24584 | tf_op jit(solution)/shard_map/ppermute | solution.py:15
  290.2 10.5 %copy-start.3 = (bf16[16,128,640]{1,2,0:T(8,128)(2,1)S(1)}, bf16[16,128,640]{1,2,0:T(8,128)(2,1)}, u32[]{:S(2)}) copy-start(bf16[16,128,640]{1,2,0:T(8,128)(2,1)} %copy-done.2) | copy-start | bytes 7864324
  295.5 192.7 %collective-permute-start.17 = (f32[128,2048]{1,0:T(8,128)}, f32[128,2048]{1,0:T(8,128)}, u32[]{:S(2)}, u32[]{:S(2)}) collective-permute-start(f32[128,2048]{1,0:T(8,128)} %copy.58), channel_id=1, source_target_pairs={{16,0},{24,8},{32,16},{40,24},{48,32},{56,40},{64,48},{72,56},{80,... | collective-permute-start | bytes 3145736 | tf_op jit(solution)/shard_map/ppermute | solution.py:15
  296.8 191.4 %collective-permute-start.18 = (f32[128,2048]{1,0:T(8,128)}, f32[128,2048]{1,0:T(8,128)}, u32[]{:S(2)}, u32[]{:S(2)}) collective-permute-start(f32[128,2048]{1,0:T(8,128)} %copy.59), channel_id=1, source_target_pairs={{24,0},{32,8},{40,16},{48,24},{56,32},{64,40},{72,48},{80,56},{88,... | collective-permute-start | bytes 3145736 | tf_op jit(solution)/shard_map/ppermute | solution.py:15
  298.1 190.1 %collective-permute-start.19 = (f32[128,2048]{1,0:T(8,128)}, f32[128,2048]{1,0:T(8,128)}, u32[]{:S(2)}, u32[]{:S(2)}) collective-permute-start(f32[128,2048]{1,0:T(8,128)} %copy.60), channel_id=1, source_target_pairs={{32,0},{40,8},{48,16},{56,24},{64,32},{72,40},{80,48},{88,56},{96,... | collective-permute-start | bytes 3145736 | tf_op jit(solution)/shard_map/ppermute | solution.py:15
  299.4 188.7 %collective-permute-start.16 = (f32[128,2048]{1,0:T(8,128)}, f32[128,2048]{1,0:T(8,128)}, u32[]{:S(2)}, u32[]{:S(2)}) collective-permute-start(f32[128,2048]{1,0:T(8,128)} %copy.56), channel_id=1, source_target_pairs={{8,0},{16,8},{24,16},{32,24},{40,32},{48,40},{56,48},{64,56},{72,6... | collective-permute-start | bytes 3145736 | tf_op jit(solution)/shard_map/ppermute | solution.py:15
  487.1 4.5 copy-start.1
  (7 other events, 16.0 us)
where the time goes:
time: 493 us; the launch traced here: 492 us
  blocking collectives  178 us (36%)
  waiting for transfers between devices  137 us (28%)
  starting transfers between devices  80.2 us (16%)
  local copies, waits for them, and re-layouts  63.1 us (13%)
  matrix products  20.4 us (4%)
  other arithmetic  10.9 us (2%)
    psum x1, blocking collectives, shards(): bias_total = lax.psum(bias_local, ('seq', 'dp'))  178 us
    ppermute x24, waiting for transfers between devices, passed_along(): lax.ppermute(value, axis, [(source, source + steps) for source in range(f...  137 us
    ppermute x24, starting transfers between devices, passed_along(): lax.ppermute(value, axis, [(source, source + steps) for source in range(f...  80.2 us
    unnamed x48, local copies, waits for them, and re-layouts  20.6 us
    slice x4, local copies, waits for them, and re-layouts, shards(): grad_key[first_row:first_row + tok_rows]  10.2 us
    slice x5, local copies, waits for them, and re-layouts, shards(): grad_value[first_row:first_row + tok_rows]  9.92 us
  transfers between devices with their start and end apart: 24, of which 5 were waited for; matrix products, arithmetic and copies ran while one was open for 8% of the time, Pallas kernels for 0%

commit v1 on v0

v1 whole, which is shorter than its diff:
```python
import functools

import jax
import jax.numpy as jnp
from jax import lax
from jax.experimental import pallas as pl
from jax.experimental.pallas import tpu as pltpu
from jax.sharding import PartitionSpec as P

HEADS = 16
HEAD_DIM = 128
WINDOW = 512
FIELDS = 64
TOK = 128
GROUP = WINDOW // TOK
LOCAL_HEADS = HEADS // GROUP
SCALE = HEAD_DIM**-0.5
LOG2E = 1.4426950408889634
MASKED = -1e30
NT = (((1,), (1,)), ((), ()))
NN = (((1,), (0,)), ((), ()))
TN = (((0,), (0,)), ((), ()))


def dot(lhs, rhs, dims):
    return lax.dot_general(lhs, rhs, dims, preferred_element_type=jnp.float32)


def kernel(
    planes,
    copies,
    length_ref,
    bias_ref,
    fields_ref,
    q_hbm,
    k_hbm,
    v_hbm,
    g_hbm,
    dq_hbm,
    dk_hbm,
    dv_hbm,
    dbias_ref,
    bias_rows,
    bias_part,
    plane_parts,
    all_parts,
    kv,
    qg,
    field_rows,
    onehot,
    key_acc,
    own_acc,
    col_acc,
    ret_src,
    ret_dst,
    out_buf,
    field_send,
    field_recv,
    field_relay,
    field_halo,
    kv_send,
    kv_recv,
    qg_send,
    qg_recv,
    halo_send,
    halo_recv,
    ret_send,
    ret_recv,
    outq_send,
    outkv_send,
    out_recv,
    plane_send,
    plane_recv,
    all_send,
    all_recv,
):
    block = lax.axis_index("seq")
    sequence = lax.axis_index("dp")
    y = lax.rem(block, GROUP)
    z = block // GROUP
    has_prev = z > 0
    has_next = z < planes - 1

    def peer(step):
        other = lax.rem(y + step, GROUP)
        return other, {"seq": z * GROUP + other}

    nxt = {"seq": block + GROUP}
    prv = {"seq": block - GROUP}

    mates = copies * GROUP
    seat = sequence * GROUP + y

    def mate(step):
        other = lax.rem(seat + step, mates)
        return {"seq": z * GROUP + lax.rem(other, GROUP), "dp": other // GROUP}

    def above(step):
        return {"seq": lax.rem(z + step, planes) * GROUP + y}

    barrier = pltpu.get_barrier_semaphore()

    @pl.loop(1, mates)
    def _(step):
        pl.semaphore_signal(barrier, inc=1, device_id=mate(step))

    @pl.loop(1, planes)
    def _(step):
        pl.semaphore_signal(barrier, inc=1, device_id=above(step))

    pl.semaphore_wait(barrier, mates + planes - 2)

    own_rows = pl.ds(pl.multiple_of(y * TOK, TOK), TOK)
    own_keys = pl.ds(pl.multiple_of(WINDOW + y * TOK, TOK), TOK)
    plane_keys = pl.ds(WINDOW, WINDOW)

    def columns(owner, head):
        return pl.ds(pl.multiple_of((owner * LOCAL_HEADS + head) * HEAD_DIM, HEAD_DIM), HEAD_DIM)

    for step in range(1, GROUP):
        pltpu.make_async_remote_copy(
            fields_ref, field_rows.at[GROUP + y], field_send, field_recv, device_id=peer(step)[1]
        ).start()
    pltpu.make_async_copy(fields_ref, field_rows.at[GROUP + y], field_recv).start()

    for head in range(LOCAL_HEADS):
        for send, recv, sources, target, rows in (
            (kv_send, kv_recv, (k_hbm, v_hbm), kv, own_keys),
            (qg_send, qg_recv, (q_hbm, g_hbm), qg, own_rows),
        ):
            for step in range(1, GROUP):
                other, device = peer(step)
                for index, source in enumerate(sources):
                    pltpu.make_async_remote_copy(
                        source.at[:, columns(other, head)],
                        target.at[head, index, rows],
                        send.at[head],
                        recv.at[head],
                        device_id=device,
                    ).start()
            for index, source in enumerate(sources):
                pltpu.make_async_copy(
                    source.at[:, columns(y, head)], target.at[head, index, rows], recv.at[head]
                ).start()

    @pl.when(jnp.logical_not(has_prev))
    def _():
        kv[:, :, 0:WINDOW, :] = jnp.zeros((LOCAL_HEADS, 2, WINDOW, HEAD_DIM), kv.dtype)
        field_rows[0:GROUP] = jnp.full((GROUP, 1, TOK), -1, jnp.int32)

    plane_fields = field_rows.at[pl.ds(GROUP, GROUP)]
    halo_fields = field_rows.at[pl.ds(0, GROUP)]
    pltpu.make_async_copy(plane_fields, plane_fields, field_recv).wait()

    @pl.when(has_next)
    def _():
        pltpu.make_async_remote_copy(
            plane_fields, halo_fields, field_relay, field_halo, device_id=nxt
        ).start()

    def relay(head):
        arrived = kv.at[head, :, plane_keys]
        pltpu.make_async_copy(arrived, arrived, kv_recv.at[head]).wait()

        @pl.when(has_next)
        def _():
            pltpu.make_async_remote_copy(
                arrived,
                kv.at[head, :, pl.ds(0, WINDOW)],
                halo_send.at[head],
                halo_recv.at[head],
                device_id=nxt,
            ).start()

    relay(0)

    @pl.when(has_prev)
    def _():
        pltpu.make_async_copy(halo_fields, halo_fields, field_halo).wait()

    lane = lax.broadcasted_iota(jnp.int32, (TOK, TOK), 1)
    row = lax.broadcasted_iota(jnp.int32, (TOK, TOK), 0)
    for part in range(2 * GROUP):
        by_lane = jnp.broadcast_to(field_rows[part].astype(jnp.float32), (TOK, TOK))
        by_row = by_lane.T
        chosen = by_row == lax.rem(lane, FIELDS).astype(jnp.float32)
        onehot[part * TOK : (part + 1) * TOK] = chosen.astype(jnp.float32).astype(jnp.bfloat16)

    field = lax.broadcasted_iota(jnp.int32, (FIELDS, 2 * FIELDS), 0)
    place = lax.broadcasted_iota(jnp.int32, (FIELDS, 2 * FIELDS), 1)
    twice = (lax.rem(place, FIELDS) == field).astype(jnp.float32).astype(jnp.bfloat16)
    scaled = dot(bias_ref[...], twice, NN) / SCALE
    high_part = scaled.astype(jnp.bfloat16).astype(jnp.float32)
    is_high = lax.broadcasted_iota(jnp.int32, (HEADS, 2 * FIELDS), 1) < FIELDS
    bias_rows[...] = jnp.where(is_high, high_part, scaled - high_part)
    bias_part[...] = jnp.zeros_like(bias_part)

    older = row > lane
    length = length_ref[0]
    unseen = jnp.where(has_prev, 0.0, MASKED)

    def work(head):
        here = qg.at[head]
        pltpu.make_async_copy(here, here, qg_recv.at[head]).wait()

        @pl.when(has_prev)
        def _():
            halo = kv.at[head, :, pl.ds(0, WINDOW)]
            pltpu.make_async_copy(halo, halo, halo_recv.at[head]).wait()

        bias_row = bias_rows[pl.ds(y * LOCAL_HEADS + head, 1), :]
        bias_block = jnp.broadcast_to(bias_row, (TOK, TOK)).astype(jnp.bfloat16)
        for part in range(GROUP):
            first = part * TOK
            span = WINDOW + TOK
            seen = pl.ds(first, span)
            queries = qg[head, 0, first : first + TOK, :]
            grads = qg[head, 1, first : first + TOK, :]
            keys = kv[head, 0, seen, :]
            values = kv[head, 1, seen, :]
            logits = dot(
                jnp.concatenate([keys, onehot[seen, :]], axis=1),
                jnp.concatenate([queries, bias_block], axis=1),
                NT,
            )
            probs_grad = dot(values, grads, NT)

            def tiles(full):
                merged = jnp.where(older, full[0:TOK], full[WINDOW:span])
                return [merged] + [full[t * TOK : (t + 1) * TOK] for t in range(1, GROUP)]

            logit_tiles = tiles(logits)
            halo_tiles = GROUP - part
            logit_tiles = [
                (jnp.where(older, tile + unseen, tile) if t == 0 else tile + unseen)
                if t < halo_tiles
                else tile
                for t, tile in enumerate(logit_tiles)
            ]
            logit = jnp.concatenate(logit_tiles, axis=0)
            peak = jnp.max(logit, axis=0, keepdims=True)
            power = jnp.exp2((logit - peak) * (SCALE * LOG2E))
            total = jnp.sum(power, axis=0, keepdims=True)
            place = z * WINDOW + first + lax.broadcasted_iota(jnp.int32, (1, TOK), 1)
            share = jnp.where(place < length, 1.0 / total, 0.0)
            weight = power * share
            weight_low = weight.astype(jnp.bfloat16)
            prob = jnp.concatenate(tiles(probs_grad), axis=0)
            delta = jnp.sum(weight_low.astype(jnp.float32) * prob, axis=0, keepdims=True)
            grad = weight * (prob - delta)

            def spread(merged):
                top = merged[0:TOK]
                none = jnp.zeros_like(top)
                return jnp.concatenate(
                    [jnp.where(older, top, none), merged[TOK:WINDOW], jnp.where(older, none, top)],
                    axis=0,
                )

            grad_full = spread(grad)
            grad_low = grad_full.astype(jnp.bfloat16)
            weight_full = spread(weight_low.astype(jnp.float32)).astype(jnp.bfloat16)
            query_grad = dot(grad_low, keys, TN) * SCALE
            out_buf[head, 0, first : first + TOK, :] = query_grad.astype(jnp.bfloat16)
            key_part = dot(grad_low, queries, NN)
            value_part = dot(weight_full, grads, NN)
            for store, fresh in ((key_acc.at[0], key_part), (key_acc.at[1], value_part), (col_acc, grad_full)):
                if part == 0:
                    store[0:span, :] = fresh
                else:
                    store[first : first + WINDOW, :] += fresh[0:WINDOW]
                    store[first + WINDOW : first + span, :] = fresh[WINDOW:span]

        ret_src[head, 0] = (key_acc[0, 0:WINDOW] * SCALE).astype(jnp.bfloat16)
        ret_src[head, 1] = key_acc[1, 0:WINDOW].astype(jnp.bfloat16)

        @pl.when(has_prev)
        def _():
            pltpu.make_async_remote_copy(
                ret_src.at[head],
                ret_dst.at[head],
                ret_send.at[head],
                ret_recv.at[head],
                device_id=prv,
            ).start()

        own_acc[head, 0] = key_acc[0, WINDOW:] * SCALE
        own_acc[head, 1] = key_acc[1, WINDOW:]

        for step in range(1, GROUP):
            other, device = peer(step)
            pltpu.make_async_remote_copy(
                out_buf.at[head, 0, pl.ds(pl.multiple_of(other * TOK, TOK), TOK)],
                dq_hbm.at[:, columns(y, head)],
                outq_send.at[head],
                out_recv.at[0],
                device_id=device,
            ).start()
        pltpu.make_async_copy(
            out_buf.at[head, 0, own_rows], dq_hbm.at[:, columns(y, head)], out_recv.at[0]
        ).start()

        sums = col_acc[...]
        high = sums.astype(jnp.bfloat16)
        low = (sums - high.astype(jnp.float32)).astype(jnp.bfloat16)
        by_query = dot(high, onehot[...], TN) + dot(low, onehot[...], TN)
        bias_part[pl.ds(head, 1), :] = jnp.sum(by_query, axis=0, keepdims=True)

    def finish(head):
        @pl.when(has_next)
        def _():
            back = ret_dst.at[head]
            pltpu.make_async_copy(back, back, ret_recv.at[head]).wait()
            for index in range(2):
                out_buf[head, 1 + index] = (
                    own_acc[head, index] + ret_dst[head, index].astype(jnp.float32)
                ).astype(jnp.bfloat16)

        @pl.when(jnp.logical_not(has_next))
        def _():
            for index in range(2):
                out_buf[head, 1 + index] = own_acc[head, index].astype(jnp.bfloat16)

        for index, result in ((1, dk_hbm), (2, dv_hbm)):
            for step in range(1, GROUP):
                other, device = peer(step)
                pltpu.make_async_remote_copy(
                    out_buf.at[head, index, pl.ds(pl.multiple_of(other * TOK, TOK), TOK)],
                    result.at[:, columns(y, head)],
                    outkv_send.at[head],
                    out_recv.at[index],
                    device_id=device,
                ).start()
            pltpu.make_async_copy(
                out_buf.at[head, index, own_rows], result.at[:, columns(y, head)], out_recv.at[index]
            ).start()

    @pl.loop(0, LOCAL_HEADS)
    def _(head):
        @pl.when(head + 1 < LOCAL_HEADS)
        def _():
            relay(head + 1)

        work(head)

        @pl.when(head == LOCAL_HEADS - 1)
        def _():
            plane_parts[seat] = bias_part[...]

            @pl.loop(1, mates)
            def _(step):
                pltpu.make_async_remote_copy(
                    bias_part, plane_parts.at[seat], plane_send, plane_recv, device_id=mate(step)
                ).start()

        @pl.when(head > 0)
        def _():
            finish(head - 1)

    others = plane_parts.at[pl.ds(0, mates - 1)]
    pltpu.make_async_copy(others, others, plane_recv).wait()
    for owner in range(GROUP):
        total = plane_parts[owner]
        for copy in range(1, copies):
            total = total + plane_parts[copy * GROUP + owner]
        first = owner * LOCAL_HEADS
        all_parts[z, first : first + LOCAL_HEADS, :] = total[0:LOCAL_HEADS]

    @pl.loop(1, planes)
    def _(step):
        mine = all_parts.at[z]
        pltpu.make_async_remote_copy(mine, mine, all_send, all_recv, device_id=above(step)).start()

    finish(LOCAL_HEADS - 1)

    rest = all_parts.at[pl.ds(0, planes - 1)]
    pltpu.make_async_copy(rest, rest, all_recv).wait()
    bias_total = all_parts[0]
    for plane in range(1, planes):
        bias_total = bias_total + all_parts[plane]
    dbias_ref[...] = bias_total[:, 0:FIELDS]

    pltpu.make_async_copy(others, others, plane_send).wait()
    pltpu.make_async_copy(rest, rest, all_send).wait()
    sent_fields = field_rows.at[pl.ds(0, GROUP - 1)]
    pltpu.make_async_copy(sent_fields, sent_fields, field_send).wait()

    @pl.when(has_next)
    def _():
        pltpu.make_async_copy(halo_fields, halo_fields, field_relay).wait()

    @pl.loop(0, LOCAL_HEADS)
    def _(head):
        sent = kv.at[head, :, pl.ds(0, WINDOW - TOK)]
        pltpu.make_async_copy(sent, sent, kv_send.at[head]).wait()
        pltpu.make_async_copy(sent, sent, qg_send.at[head]).wait()
        pltpu.make_async_copy(sent, sent, outkv_send.at[head]).wait()
        query_sent = kv.at[head, 0, pl.ds(0, WINDOW - TOK)]
        pltpu.make_async_copy(query_sent, query_sent, outq_send.at[head]).wait()

        @pl.when(has_next)
        def _():
            halo = kv.at[head, :, pl.ds(0, WINDOW)]
            pltpu.make_async_copy(halo, halo, halo_send.at[head]).wait()

        @pl.when(has_prev)
        def _():
            source = ret_src.at[head]
            pltpu.make_async_copy(source, source, ret_send.at[head]).wait()

    for index, result in enumerate((dq_hbm, dk_hbm, dv_hbm)):
        pltpu.make_async_copy(result, result, out_recv.at[index]).wait()


def copy_kernel(*refs):
    count = len(refs) // 2
    sources, targets, sems = refs[:count], refs[count : 2 * count], refs[-1]
    moves = [
        pltpu.make_async_copy(sources[index], targets[index], sems.at[index]) for index in range(count)
    ]
    for move in moves:
        move.start()
    for move in moves:
        move.wait()


def shards(planes, copies, queries, keys, values, grad_out, lengths, fields, field_bias):
    tok_rows, row_width = queries.shape[1:]
    low_type, full_type = jnp.bfloat16, jnp.float32
    grads_shape = jax.ShapeDtypeStruct((tok_rows, row_width), low_type)
    anywhere = pl.BlockSpec(memory_space=pl.ANY)
    in_vmem = pl.BlockSpec(memory_space=pltpu.VMEM)
    dma = pltpu.SemaphoreType.DMA
    heads = LOCAL_HEADS
    query_grad, key_grad, value_grad, bias_total = pl.pallas_call(
        functools.partial(kernel, planes, copies),
        out_shape=(
            grads_shape,
            grads_shape,
            grads_shape,
            jax.ShapeDtypeStruct((HEADS, FIELDS), full_type),
        ),
        in_specs=[
            pl.BlockSpec(memory_space=pltpu.SMEM),
            in_vmem,
            in_vmem,
            anywhere,
            anywhere,
            anywhere,
            anywhere,
        ],
        out_specs=(anywhere, anywhere, anywhere, in_vmem),
        scratch_shapes=[
            pltpu.VMEM((HEADS, 2 * FIELDS), full_type),
            pltpu.VMEM((8, 2 * FIELDS), full_type),
            pltpu.VMEM((copies * GROUP, 8, 2 * FIELDS), full_type),
            pltpu.VMEM((planes, HEADS, 2 * FIELDS), full_type),
            pltpu.VMEM((heads, 2, 2 * WINDOW, HEAD_DIM), low_type),
            pltpu.VMEM((heads, 2, WINDOW, HEAD_DIM), low_type),
            pltpu.VMEM((2 * GROUP, 1, TOK), jnp.int32),
            pltpu.VMEM((2 * WINDOW, 2 * FIELDS), low_type),
            pltpu.VMEM((2, 2 * WINDOW, HEAD_DIM), full_type),
            pltpu.VMEM((heads, 2, WINDOW, HEAD_DIM), full_type),
            pltpu.VMEM((2 * WINDOW, HEAD_DIM), full_type),
            pltpu.VMEM((heads, 2, WINDOW, HEAD_DIM), low_type),
            pltpu.VMEM((heads, 2, WINDOW, HEAD_DIM), low_type),
            pltpu.VMEM((heads, 3, WINDOW, HEAD_DIM), low_type),
            dma,
            dma,
            dma,
            dma,
            dma((heads,)),
            dma((heads,)),
            dma((heads,)),
            dma((heads,)),
            dma((heads,)),
            dma((heads,)),
            dma((heads,)),
            dma((heads,)),
            dma((heads,)),
            dma((heads,)),
            dma((3,)),
            dma,
            dma,
            dma,
            dma,
        ],
        compiler_params=pltpu.CompilerParams(
            collective_id=0, has_side_effects=True, vmem_limit_bytes=56 * 2**20
        ),
    )(lengths, field_bias, fields, queries[0], keys[0], values[0], grad_out[0])
    results = (query_grad, key_grad, value_grad, bias_total)
    query_grad, key_grad, value_grad, bias_total = pl.pallas_call(
        copy_kernel,
        out_shape=tuple(jax.ShapeDtypeStruct(one.shape, one.dtype) for one in results),
        in_specs=[anywhere] * 4,
        out_specs=(anywhere,) * 4,
        scratch_shapes=[dma((4,))],
        compiler_params=pltpu.CompilerParams(vmem_limit_bytes=56 * 2**20),
    )(*results)
    return query_grad[None], key_grad[None], value_grad[None], bias_total


def solution(mesh):
    rows = P("dp", "seq", None)
    return jax.shard_map(
        functools.partial(shards, mesh.shape["seq"] // GROUP, mesh.shape["dp"]),
        mesh=mesh,
        in_specs=(rows, rows, rows, rows, P("dp"), P("dp", "seq"), P()),
        out_specs=(rows, rows, rows, P()),
        check_vma=False,
    )
```

time: 493 us -> 117 us (0.24)
  blocking collectives: 178 us -> 0 us
  waiting for transfers between devices: 137 us -> 0 us
  Pallas kernels: 0 us -> 115 us
  starting transfers between devices: 80.2 us -> 0 us
  local copies, waits for them, and re-layouts: 63.1 us -> 0 us
  matrix products: 20.4 us -> 0 us
  other arithmetic: 10.9 us -> 0 us
    psum x1 -> x0, blocking collectives: 178 us -> none  [shards(): bias_total = lax.psum(bias_local, ('seq', 'dp'))]
    ppermute x24 -> x0, waiting for transfers between devices: 137 us -> none  [passed_along(): lax.ppermute(value, axis, [(source, source + steps) for source in range(f...]
    pallas_call x0 -> x2, Pallas kernels: none -> 115 us  [the longest x1 66.2 us: shards(): pl.pallas_call(functools.partial(kernel, planes, copies), out_shape=(grad...]
    ppermute x24 -> x0, starting transfers between devices: 80.2 us -> none  [passed_along(): lax.ppermute(value, axis, [(source, source + steps) for source in range(f...]
    slice x13 -> x0, local copies, waits for them, and re-layouts: 24.4 us -> none  [the longest x4 10.2 us: shards(): grad_key[first_row:first_row + tok_rows]]
    unnamed x48 -> x0, local copies, waits for them, and re-layouts: 20.6 us -> none
    concatenate x13 -> x0, local copies, waits for them, and re-layouts: 15.7 us -> none  [the longest x6 9.36 us: shards(): key_all = jnp.concatenate([arrival[0] for arrival in ordered], axis=0)]
    dot_general x7 -> x0, matrix products: 12.8 us -> none  [the longest x1 5.15 us: grad_logits_of(): jnp.einsum('qhd,khd->hqk', grad_heads, value_heads, preferred_element_typ...]
  transfers between devices with their start and end apart: 24 -> 0, of which waited for: 5 -> 0; matrix products, arithmetic and copies ran while one was open for 8% -> 0% of each run, Pallas kernels for 0% -> 0%
where the time goes in v1:
time: 117 us
  Pallas kernels  115 us (98%)
  between operations  1.29 us (1%)
    pallas_call x1, Pallas kernels, shards(): pl.pallas_call(functools.partial(kernel, planes, copies), out_shape=(grad...  66.2 us
    pallas_call x1, Pallas kernels, shards(): pl.pallas_call(copy_kernel, out_shape=tuple((jax.ShapeDtypeStruct(one.sha...  49 us

profile of v1, /device:TPU:1, one launch (start us, length us, event | category | flops | bytes accessed | tf_op | source)
XLA Modules:
  0.0 116.6 jit_solution(8844842031403458642)
XLA Ops:
  1.3 66.2 %shard_map.102 = (bf16[128,2048]{1,0:T(8,128)(2,1)}, bf16[128,2048]{1,0:T(8,128)(2,1)}, bf16[128,2048]{1,0:T(8,128)(2,1)}, f32[16,64]{1,0:T(8,128)}) custom-call(s32[1]{0:T(128)S(6)} %copy.11.length_ref, bf16[16,64]{1,0:T(8,128)(2,1)} %bias_ref.1, s32[1,128]{1,0:T(1,128)} %fields_ref.1, bf16[128,2048]{1,0:T(8,128)(2,1)} %bitcast.7, ...), custom_call_target="tpu_custom_call" | custom-call | tf_op jit(solution)/shard_map/pallas_call | solution.py:435
  67.5 49.0 %shard_map.103 = (bf16[128,2048]{1,0:T(8,128)(2,1)}, bf16[128,2048]{1,0:T(8,128)(2,1)}, bf16[128,2048]{1,0:T(8,128)(2,1)}, f32[16,64]{1,0:T(8,128)}) custom-call(bf16[128,2048]{1,0:T(8,128)(2,1)} %get-tuple-element.12.refs_0_, bf16[128,2048]{1,0:T(8,128)(2,1)} %get-tuple-element.13.refs_1_, bf16[128,2048]{1,0:T(8,128)(2,1)} %get-tuple-element.14.refs_2_, ...), custom_call_target="tpu_custom_call" | custom-call | tf_op jit(solution)/shard_map/pallas_call | solution.py:493

commit v2 on v1

--- a/solution.py
+++ b/solution.py
@@ -36,9 +36,9 @@
     k_hbm,
     v_hbm,
     g_hbm,
-    dq_hbm,
-    dk_hbm,
-    dv_hbm,
+    dq_ref,
+    dk_ref,
+    dv_ref,
     dbias_ref,
     bias_rows,
     bias_part,
@@ -291,13 +291,13 @@
             other, device = peer(step)
             pltpu.make_async_remote_copy(
                 out_buf.at[head, 0, pl.ds(pl.multiple_of(other * TOK, TOK), TOK)],
-                dq_hbm.at[:, columns(y, head)],
+                dq_ref.at[:, columns(y, head)],
                 outq_send.at[head],
                 out_recv.at[0],
                 device_id=device,
             ).start()
         pltpu.make_async_copy(
-            out_buf.at[head, 0, own_rows], dq_hbm.at[:, columns(y, head)], out_recv.at[0]
+            out_buf.at[head, 0, own_rows], dq_ref.at[:, columns(y, head)], out_recv.at[0]
         ).start()
 
         sums = col_acc[...]
@@ -321,7 +321,7 @@
             for index in range(2):
                 out_buf[head, 1 + index] = own_acc[head, index].astype(jnp.bfloat16)
 
-        for index, result in ((1, dk_hbm), (2, dv_hbm)):
+        for index, result in ((1, dk_ref), (2, dv_ref)):
             for step in range(1, GROUP):
                 other, device = peer(step)
                 pltpu.make_async_remote_copy(
@@ -408,7 +408,7 @@
             source = ret_src.at[head]
             pltpu.make_async_copy(source, source, ret_send.at[head]).wait()
 
-    for index, result in enumerate((dq_hbm, dk_hbm, dv_hbm)):
+    for index, result in enumerate((dq_ref, dk_ref, dv_ref)):
         pltpu.make_async_copy(result, result, out_recv.at[index]).wait()
 
 
@@ -428,28 +428,28 @@
     tok_rows, row_width = queries.shape[1:]
     low_type, full_type = jnp.bfloat16, jnp.float32
     grads_shape = jax.ShapeDtypeStruct((tok_rows, row_width), low_type)
-    anywhere = pl.BlockSpec(memory_space=pl.ANY)
+    in_hbm = pl.BlockSpec(memory_space=pltpu.HBM)
     in_vmem = pl.BlockSpec(memory_space=pltpu.VMEM)
     dma = pltpu.SemaphoreType.DMA
     heads = LOCAL_HEADS
     query_grad, key_grad, value_grad, bias_total = pl.pallas_call(
         functools.partial(kernel, planes, copies),
         out_shape=(
-            grads_shape,
-            grads_shape,
-            grads_shape,
-            jax.ShapeDtypeStruct((HEADS, FIELDS), full_type),
+            pltpu.VMEM(grads_shape.shape, low_type),
+            pltpu.VMEM(grads_shape.shape, low_type),
+            pltpu.VMEM(grads_shape.shape, low_type),
+            pltpu.VMEM((HEADS, FIELDS), full_type),
         ),
         in_specs=[
             pl.BlockSpec(memory_space=pltpu.SMEM),
             in_vmem,
             in_vmem,
-            anywhere,
-            anywhere,
-            anywhere,
-            anywhere,
+            in_hbm,
+            in_hbm,
+            in_hbm,
+            in_hbm,
         ],
-        out_specs=(anywhere, anywhere, anywhere, in_vmem),
+        out_specs=(in_vmem, in_vmem, in_vmem, in_vmem),
         scratch_shapes=[
             pltpu.VMEM((HEADS, 2 * FIELDS), full_type),
             pltpu.VMEM((8, 2 * FIELDS), full_type),
@@ -486,17 +486,17 @@
             dma,
         ],
         compiler_params=pltpu.CompilerParams(
-            collective_id=0, has_side_effects=True, vmem_limit_bytes=56 * 2**20
+            collective_id=0, has_side_effects=True, vmem_limit_bytes=60 * 2**20
         ),
     )(lengths, field_bias, fields, queries[0], keys[0], values[0], grad_out[0])
     results = (query_grad, key_grad, value_grad, bias_total)
     query_grad, key_grad, value_grad, bias_total = pl.pallas_call(
         copy_kernel,
         out_shape=tuple(jax.ShapeDtypeStruct(one.shape, one.dtype) for one in results),
-        in_specs=[anywhere] * 4,
-        out_specs=(anywhere,) * 4,
+        in_specs=[in_vmem] * 4,
+        out_specs=(in_hbm,) * 4,
         scratch_shapes=[dma((4,))],
-        compiler_params=pltpu.CompilerParams(vmem_limit_bytes=56 * 2**20),
+        compiler_params=pltpu.CompilerParams(vmem_limit_bytes=2**20),
     )(*results)
     return query_grad[None], key_grad[None], value_grad[None], bias_total
 

time: 117 us -> 68.2 us (0.58)
  Pallas kernels: 115 us -> 66.7 us
    pallas_call x1, Pallas kernels: 49 us -> 1.18 us  [shards(): pl.pallas_call(copy_kernel, out_shape=tuple((jax.ShapeDtypeStruct(one.sha...]
where the time goes in v2:
time: 68.2 us; the launch traced here: 68 us
  Pallas kernels  66.7 us (98%)
  between operations  1.29 us (2%)
    pallas_call x1, Pallas kernels, shards(): pl.pallas_call(functools.partial(kernel, planes, copies), out_shape=(pltp...  65.5 us

profile of v2, /device:TPU:1, one launch (start us, length us, event | category | flops | bytes accessed | tf_op | source)
XLA Modules:
  0.0 68.0 jit_solution(82886998734482258)
XLA Ops:
  1.3 65.5 %shard_map.102 = (bf16[128,2048]{1,0:T(8,128)(2,1)S(1)}, bf16[128,2048]{1,0:T(8,128)(2,1)S(1)}, bf16[128,2048]{1,0:T(8,128)(2,1)S(1)}, f32[16,64]{1,0:T(8,128)S(1)}) custom-call(s32[1]{0:T(128)S(6)} %copy.11.length_ref, bf16[16,64]{1,0:T(8,128)(2,1)} %bias_ref.1, s32[1,128]{1,0:T(1,128)} %fields_ref.1, bf16[128,2048]{1,0:T(8,128)(2,1)} %bitcast.7, ...), custom_call_target="tpu_custom_call" | custom-call | tf_op jit(solution)/shard_map/pallas_call | solution.py:435
  66.8 1.2 %shard_map.103 = (bf16[128,2048]{1,0:T(8,128)(2,1)}, bf16[128,2048]{1,0:T(8,128)(2,1)}, bf16[128,2048]{1,0:T(8,128)(2,1)}, f32[16,64]{1,0:T(8,128)}) custom-call(bf16[128,2048]{1,0:T(8,128)(2,1)S(1)} %get-tuple-element.12.refs_0_, bf16[128,2048]{1,0:T(8,128)(2,1)S(1)} %get-tuple-element.13.refs_1_, bf16[128,2048]{1,0:T(8,128)(2,1)S(1)} %get-tuple-element.14.refs_2_, ...), custom_call_target="tpu_custom_call" | custom-call | tf_op jit(solution)/shard_map/pallas_call | solution.py:493

commit v3 on v2

--- a/solution.py
+++ b/solution.py
@@ -42,8 +42,9 @@
     dbias_ref,
     bias_rows,
     bias_part,
+    mine,
     plane_parts,
-    all_parts,
+    mate_parts,
     kv,
     qg,
     field_rows,
@@ -71,8 +72,10 @@
     out_recv,
     plane_send,
     plane_recv,
-    all_send,
-    all_recv,
+    mate_send,
+    mate_recv,
+    rows_ready,
+    known,
 ):
     block = lax.axis_index("seq")
     sequence = lax.axis_index("dp")
@@ -91,57 +94,99 @@
     mates = copies * GROUP
     seat = sequence * GROUP + y
 
-    def mate(step):
-        other = lax.rem(seat + step, mates)
-        return {"seq": z * GROUP + lax.rem(other, GROUP), "dp": other // GROUP}
-
-    def above(step):
-        return {"seq": lax.rem(z + step, planes) * GROUP + y}
+    def at_distance(distance, act):
+        @pl.when(z >= distance)
+        def _():
+            act(block - distance * GROUP)
+
+        @pl.when(z + distance < planes)
+        def _():
+            act(block + distance * GROUP)
+
+    def count_at(distance):
+        below = (z >= distance).astype(jnp.int32)
+        return below + (z + distance < planes).astype(jnp.int32)
 
     barrier = pltpu.get_barrier_semaphore()
 
-    @pl.loop(1, mates)
-    def _(step):
-        pl.semaphore_signal(barrier, inc=1, device_id=mate(step))
-
-    @pl.loop(1, planes)
-    def _(step):
-        pl.semaphore_signal(barrier, inc=1, device_id=above(step))
-
-    pl.semaphore_wait(barrier, mates + planes - 2)
-
+    def greet(other):
+        pl.semaphore_signal(barrier, inc=1, device_id={"seq": other})
+
+    def twin(step):
+        return {"dp": lax.rem(sequence + step, copies)}
+
+    for step in range(1, GROUP):
+        pl.semaphore_signal(barrier, inc=1, device_id=peer(step)[1])
+    at_distance(1, greet)
+    for step in range(1, copies):
+        pl.semaphore_signal(barrier, inc=1, device_id=twin(step))
     own_rows = pl.ds(pl.multiple_of(y * TOK, TOK), TOK)
     own_keys = pl.ds(pl.multiple_of(WINDOW + y * TOK, TOK), TOK)
     plane_keys = pl.ds(WINDOW, WINDOW)
 
     def columns(owner, head):
         return pl.ds(pl.multiple_of((owner * LOCAL_HEADS + head) * HEAD_DIM, HEAD_DIM), HEAD_DIM)
+
+    arrays = ((kv_send, kv_recv, (k_hbm, v_hbm), kv, own_keys), (qg_send, qg_recv, (q_hbm, g_hbm), qg, own_rows))
+
+    pltpu.make_async_copy(fields_ref, field_rows.at[GROUP + y], field_recv).start()
+    for head in range(LOCAL_HEADS):
+        for _, recv, sources, target, rows in arrays:
+            for index, source in enumerate(sources):
+                pltpu.make_async_copy(
+                    source.at[:, columns(y, head)], target.at[head, index, rows], recv.at[head, y]
+                ).start()
+
+    pl.semaphore_wait(barrier, GROUP + copies - 2 + count_at(1))
+
+    def give(kind, head):
+        send, recv, sources, target, rows = arrays[kind]
+        for step in range(1, GROUP):
+            other, device = peer(step)
+            for index, source in enumerate(sources):
+                pltpu.make_async_remote_copy(
+                    source.at[:, columns(other, head)],
+                    target.at[head, index, rows],
+                    send.at[head],
+                    recv.at[head, y],
+                    device_id=device,
+                ).start()
+
+    give(0, 0)
+
+    @pl.when(has_next)
+    def _():
+        for head in range(LOCAL_HEADS):
+            for index, source in enumerate((k_hbm, v_hbm)):
+                pltpu.make_async_remote_copy(
+                    source.at[:, columns(y, head)],
+                    kv.at[head, index, own_rows],
+                    halo_send.at[head],
+                    halo_recv.at[head, y],
+                    device_id=nxt,
+                ).start()
 
     for step in range(1, GROUP):
         pltpu.make_async_remote_copy(
             fields_ref, field_rows.at[GROUP + y], field_send, field_recv, device_id=peer(step)[1]
         ).start()
-    pltpu.make_async_copy(fields_ref, field_rows.at[GROUP + y], field_recv).start()
-
-    for head in range(LOCAL_HEADS):
-        for send, recv, sources, target, rows in (
-            (kv_send, kv_recv, (k_hbm, v_hbm), kv, own_keys),
-            (qg_send, qg_recv, (q_hbm, g_hbm), qg, own_rows),
-        ):
-            for step in range(1, GROUP):
-                other, device = peer(step)
-                for index, source in enumerate(sources):
-                    pltpu.make_async_remote_copy(
-                        source.at[:, columns(other, head)],
-                        target.at[head, index, rows],
-                        send.at[head],
-                        recv.at[head],
-                        device_id=device,
-                    ).start()
-            for index, source in enumerate(sources):
-                pltpu.make_async_copy(
-                    source.at[:, columns(y, head)], target.at[head, index, rows], recv.at[head]
-                ).start()
+    give(0, 1)
+    give(1, 0)
+
+    for step in range(1, copies):
+        pl.semaphore_signal(rows_ready, inc=1, device_id=twin(step))
+
+    def tell(turn):
+        def act(other):
+            pl.semaphore_signal(known.at[turn], inc=1, device_id={"seq": other})
+
+        at_distance(2**turn, act)
+
+    def hear(turn):
+        pl.semaphore_wait(known.at[turn], count_at(2**turn))
+
+    turns = (planes - 1).bit_length()
+    tell(0)
 
     @pl.when(jnp.logical_not(has_prev))
     def _():
@@ -158,21 +203,29 @@
             plane_fields, halo_fields, field_relay, field_halo, device_id=nxt
         ).start()
 
+    def block_rows(first, source):
+        return pl.ds(pl.multiple_of(first + source * TOK, TOK), TOK)
+
     def relay(head):
-        arrived = kv.at[head, :, plane_keys]
-        pltpu.make_async_copy(arrived, arrived, kv_recv.at[head]).wait()
-
-        @pl.when(has_next)
-        def _():
-            pltpu.make_async_remote_copy(
-                arrived,
-                kv.at[head, :, pl.ds(0, WINDOW)],
-                halo_send.at[head],
-                halo_recv.at[head],
-                device_id=nxt,
-            ).start()
+        own = kv.at[head, :, own_keys]
+        pltpu.make_async_copy(own, own, kv_recv.at[head, y]).wait()
+        for step in range(1, GROUP):
+            source = lax.rem(y + GROUP - step, GROUP)
+            arrived = kv.at[head, :, block_rows(WINDOW, source)]
+            pltpu.make_async_copy(arrived, arrived, kv_recv.at[head, source]).wait()
+
+            @pl.when(has_next)
+            def _():
+                pltpu.make_async_remote_copy(
+                    arrived,
+                    kv.at[head, :, block_rows(0, source)],
+                    halo_send.at[head],
+                    halo_recv.at[head, source],
+                    device_id=nxt,
+                ).start()
 
     relay(0)
+    give(0, 2)
 
     @pl.when(has_prev)
     def _():
@@ -193,20 +246,17 @@
     high_part = scaled.astype(jnp.bfloat16).astype(jnp.float32)
     is_high = lax.broadcasted_iota(jnp.int32, (HEADS, 2 * FIELDS), 1) < FIELDS
     bias_rows[...] = jnp.where(is_high, high_part, scaled - high_part)
-    bias_part[...] = jnp.zeros_like(bias_part)
 
     older = row > lane
     length = length_ref[0]
     unseen = jnp.where(has_prev, 0.0, MASKED)
 
     def work(head):
-        here = qg.at[head]
-        pltpu.make_async_copy(here, here, qg_recv.at[head]).wait()
-
         @pl.when(has_prev)
         def _():
-            halo = kv.at[head, :, pl.ds(0, WINDOW)]
-            pltpu.make_async_copy(halo, halo, halo_recv.at[head]).wait()
+            for source in range(GROUP):
+                halo = kv.at[head, :, pl.ds(source * TOK, TOK)]
+                pltpu.make_async_copy(halo, halo, halo_recv.at[head, source]).wait()
 
         bias_row = bias_rows[pl.ds(y * LOCAL_HEADS + head, 1), :]
         bias_block = jnp.broadcast_to(bias_row, (TOK, TOK)).astype(jnp.bfloat16)
@@ -214,6 +264,8 @@
             first = part * TOK
             span = WINDOW + TOK
             seen = pl.ds(first, span)
+            here = qg.at[head, :, pl.ds(first, TOK)]
+            pltpu.make_async_copy(here, here, qg_recv.at[head, part]).wait()
             queries = qg[head, 0, first : first + TOK, :]
             grads = qg[head, 1, first : first + TOK, :]
             keys = kv[head, 0, seen, :]
@@ -271,6 +323,17 @@
                     store[first : first + WINDOW, :] += fresh[0:WINDOW]
                     store[first + WINDOW : first + span, :] = fresh[WINDOW:span]
 
+        own_acc[head, 0] = key_acc[0, WINDOW:] * SCALE
+        own_acc[head, 1] = key_acc[1, WINDOW:]
+
+
+        sums = col_acc[...]
+        high = sums.astype(jnp.bfloat16)
+        low = (sums - high.astype(jnp.float32)).astype(jnp.bfloat16)
+        by_query = dot(high, onehot[...], TN) + dot(low, onehot[...], TN)
+        bias_part[head] = jnp.sum(by_query, axis=0, keepdims=True)
+
+    def give_back(head):
         ret_src[head, 0] = (key_acc[0, 0:WINDOW] * SCALE).astype(jnp.bfloat16)
         ret_src[head, 1] = key_acc[1, 0:WINDOW].astype(jnp.bfloat16)
 
@@ -284,9 +347,7 @@
                 device_id=prv,
             ).start()
 
-        own_acc[head, 0] = key_acc[0, WINDOW:] * SCALE
-        own_acc[head, 1] = key_acc[1, WINDOW:]
-
+    def give_query(head):
         for step in range(1, GROUP):
             other, device = peer(step)
             pltpu.make_async_remote_copy(
@@ -299,12 +360,6 @@
         pltpu.make_async_copy(
             out_buf.at[head, 0, own_rows], dq_ref.at[:, columns(y, head)], out_recv.at[0]
         ).start()
-
-        sums = col_acc[...]
-        high = sums.astype(jnp.bfloat16)
-        low = (sums - high.astype(jnp.float32)).astype(jnp.bfloat16)
-        by_query = dot(high, onehot[...], TN) + dot(low, onehot[...], TN)
-        bias_part[pl.ds(head, 1), :] = jnp.sum(by_query, axis=0, keepdims=True)
 
     def finish(head):
         @pl.when(has_next)
@@ -335,53 +390,83 @@
                 out_buf.at[head, index, own_rows], result.at[:, columns(y, head)], out_recv.at[index]
             ).start()
 
+    hear(0)
+    tell(1)
+    relay(1)
+    give(0, 3)
+    give(1, 1)
+
     @pl.loop(0, LOCAL_HEADS)
     def _(head):
-        @pl.when(head + 1 < LOCAL_HEADS)
-        def _():
-            relay(head + 1)
+        for turn in range(1, turns - 1):
+
+            @pl.when(head == min(turn - 1, LOCAL_HEADS - 1))
+            def _():
+                hear(turn)
+                tell(turn + 1)
 
         work(head)
 
+        @pl.when(head == 0)
+        def _():
+            for later in range(2, LOCAL_HEADS):
+                relay(later)
+                give(1, later)
+
         @pl.when(head == LOCAL_HEADS - 1)
         def _():
-            plane_parts[seat] = bias_part[...]
-
-            @pl.loop(1, mates)
+            for pair in range(LOCAL_HEADS // 2):
+                mine[pair] = jnp.where(is_high[0:1], bias_part[2 * pair], bias_part[2 * pair + 1])
+            plane_parts[z] = mine[...]
+            hear(turns - 1)
+
+            @pl.loop(0, planes - 1)
             def _(step):
+                target = step + (step >= z).astype(jnp.int32)
                 pltpu.make_async_remote_copy(
-                    bias_part, plane_parts.at[seat], plane_send, plane_recv, device_id=mate(step)
+                    mine,
+                    plane_parts.at[z],
+                    plane_send,
+                    plane_recv,
+                    device_id={"seq": target * GROUP + y},
                 ).start()
 
-        @pl.when(head > 0)
-        def _():
-            finish(head - 1)
-
-    others = plane_parts.at[pl.ds(0, mates - 1)]
-    pltpu.make_async_copy(others, others, plane_recv).wait()
-    for owner in range(GROUP):
-        total = plane_parts[owner]
-        for copy in range(1, copies):
-            total = total + plane_parts[copy * GROUP + owner]
-        first = owner * LOCAL_HEADS
-        all_parts[z, first : first + LOCAL_HEADS, :] = total[0:LOCAL_HEADS]
-
-    @pl.loop(1, planes)
+        give_back(head)
+
+    def rest_of(parts):
+        return parts.at[pl.ds(0, parts.shape[0] - 1)]
+
+    def landed(parts, sem):
+        pltpu.make_async_copy(rest_of(parts), rest_of(parts), sem).wait()
+
+    def sum_of(parts):
+        total = parts[0]
+        for index in range(1, parts.shape[0]):
+            total = total + parts[index]
+        return total
+
+    for head in range(LOCAL_HEADS):
+        give_query(head)
+        finish(head)
+
+    landed(plane_parts, plane_recv)
+    mate_parts[seat] = sum_of(plane_parts)
+    pl.semaphore_wait(rows_ready, copies - 1)
+
+    @pl.loop(1, mates)
     def _(step):
-        mine = all_parts.at[z]
-        pltpu.make_async_remote_copy(mine, mine, all_send, all_recv, device_id=above(step)).start()
-
-    finish(LOCAL_HEADS - 1)
-
-    rest = all_parts.at[pl.ds(0, planes - 1)]
-    pltpu.make_async_copy(rest, rest, all_recv).wait()
-    bias_total = all_parts[0]
-    for plane in range(1, planes):
-        bias_total = bias_total + all_parts[plane]
-    dbias_ref[...] = bias_total[:, 0:FIELDS]
-
-    pltpu.make_async_copy(others, others, plane_send).wait()
-    pltpu.make_async_copy(rest, rest, all_send).wait()
+        other = lax.rem(seat + step, mates)
+        part = mate_parts.at[seat]
+        pltpu.make_async_remote_copy(
+            part,
+            part,
+            mate_send,
+            mate_recv,
+            device_id={"seq": z * GROUP + lax.rem(other, GROUP), "dp": other // GROUP},
+        ).start()
+
+    for parts, sem in ((plane_parts, plane_send), (mate_parts, mate_send)):
+        landed(parts, sem)
     sent_fields = field_rows.at[pl.ds(0, GROUP - 1)]
     pltpu.make_async_copy(sent_fields, sent_fields, field_send).wait()
 
@@ -410,6 +495,16 @@
 
     for index, result in enumerate((dq_ref, dk_ref, dv_ref)):
         pltpu.make_async_copy(result, result, out_recv.at[index]).wait()
+
+    landed(mate_parts, mate_recv)
+    for owner in range(GROUP):
+        for pair in range(LOCAL_HEADS // 2):
+            both = mate_parts[owner, pair]
+            for copy in range(1, copies):
+                both = both + mate_parts[copy * GROUP + owner, pair]
+            first = owner * LOCAL_HEADS + 2 * pair
+            dbias_ref[first : first + 1, :] = both[:, 0:FIELDS]
+            dbias_ref[first + 1 : first + 2, :] = pltpu.roll(both, FIELDS, 1)[:, 0:FIELDS]
 
 
 def copy_kernel(*refs):
@@ -452,9 +547,10 @@
         out_specs=(in_vmem, in_vmem, in_vmem, in_vmem),
         scratch_shapes=[
             pltpu.VMEM((HEADS, 2 * FIELDS), full_type),
-            pltpu.VMEM((8, 2 * FIELDS), full_type),
-            pltpu.VMEM((copies * GROUP, 8, 2 * FIELDS), full_type),
-            pltpu.VMEM((planes, HEADS, 2 * FIELDS), full_type),
+            pltpu.VMEM((heads, 1, 2 * FIELDS), full_type),
+            pltpu.VMEM((heads // 2, 1, 2 * FIELDS), full_type),
+            pltpu.VMEM((planes, heads // 2, 1, 2 * FIELDS), full_type),
+            pltpu.VMEM((copies * GROUP, heads // 2, 1, 2 * FIELDS), full_type),
             pltpu.VMEM((heads, 2, 2 * WINDOW, HEAD_DIM), low_type),
             pltpu.VMEM((heads, 2, WINDOW, HEAD_DIM), low_type),
             pltpu.VMEM((2 * GROUP, 1, TOK), jnp.int32),
@@ -470,11 +566,11 @@
             dma,
             dma,
             dma((heads,)),
+            dma((heads, GROUP)),
             dma((heads,)),
+            dma((heads, GROUP)),
             dma((heads,)),
-            dma((heads,)),
-            dma((heads,)),
-            dma((heads,)),
+            dma((heads, GROUP)),
             dma((heads,)),
             dma((heads,)),
             dma((heads,)),
@@ -484,6 +580,8 @@
             dma,
             dma,
             dma,
+            pltpu.SemaphoreType.REGULAR,
+            pltpu.SemaphoreType.REGULAR(((planes - 1).bit_length(),)),
         ],
         compiler_params=pltpu.CompilerParams(
             collective_id=0, has_side_effects=True, vmem_limit_bytes=60 * 2**20

time: 68.2 us -> 64.1 us (0.940)
  Pallas kernels: 66.7 us -> 62.1 us
    pallas_call x1, Pallas kernels: 65.5 us -> 60.9 us  [shards(): pl.pallas_call(functools.partial(kernel, planes, copies), out_shape=(pltp...]
where the time goes in v3:
time: 64.1 us; the launch traced here: 63.4 us
  Pallas kernels  62.1 us (97%)
  between operations  1.29 us (2%)
    pallas_call x1, Pallas kernels, shards(): pl.pallas_call(functools.partial(kernel, planes, copies), out_shape=(pltp...  60.9 us

profile of v3, /device:TPU:1, one launch (start us, length us, event | category | flops | bytes accessed | tf_op | source)
XLA Modules:
  0.0 63.4 jit_solution(3225052439605774094)
XLA Ops:
  1.3 60.9 %shard_map.102 = (bf16[128,2048]{1,0:T(8,128)(2,1)S(1)}, bf16[128,2048]{1,0:T(8,128)(2,1)S(1)}, bf16[128,2048]{1,0:T(8,128)(2,1)S(1)}, f32[16,64]{1,0:T(8,128)S(1)}) custom-call(s32[1]{0:T(128)S(6)} %copy.11.length_ref, bf16[16,64]{1,0:T(8,128)(2,1)} %bias_ref.1, s32[1,128]{1,0:T(1,128)} %fields_ref.1, bf16[128,2048]{1,0:T(8,128)(2,1)} %bitcast.7, ...), custom_call_target="tpu_custom_call" | custom-call | tf_op jit(solution)/shard_map/pallas_call | solution.py:530
  62.2 1.2 %shard_map.103 = (bf16[128,2048]{1,0:T(8,128)(2,1)}, bf16[128,2048]{1,0:T(8,128)(2,1)}, bf16[128,2048]{1,0:T(8,128)(2,1)}, f32[16,64]{1,0:T(8,128)}) custom-call(bf16[128,2048]{1,0:T(8,128)(2,1)S(1)} %get-tuple-element.12.refs_0_, bf16[128,2048]{1,0:T(8,128)(2,1)S(1)} %get-tuple-element.13.refs_1_, bf16[128,2048]{1,0:T(8,128)(2,1)S(1)} %get-tuple-element.14.refs_2_, ...), custom_call_target="tpu_custom_call" | custom-call | tf_op jit(solution)/shard_map/pallas_call | solution.py:591

commit v4 on v3

--- a/solution.py
+++ b/solution.py
@@ -49,6 +49,7 @@
     qg,
     field_rows,
     onehot,
+    field_of_key,
     key_acc,
     own_acc,
     col_acc,
@@ -236,6 +237,8 @@
     for part in range(2 * GROUP):
         by_lane = jnp.broadcast_to(field_rows[part].astype(jnp.float32), (TOK, TOK))
         by_row = by_lane.T
+        by_field = by_lane == lax.rem(row, FIELDS).astype(jnp.float32)
+        field_of_key[:, part * TOK : (part + 1) * TOK] = by_field.astype(jnp.float32).astype(jnp.bfloat16)
         chosen = by_row == lax.rem(lane, FIELDS).astype(jnp.float32)
         onehot[part * TOK : (part + 1) * TOK] = chosen.astype(jnp.float32).astype(jnp.bfloat16)
 
@@ -248,10 +251,16 @@
     bias_rows[...] = jnp.where(is_high, high_part, scaled - high_part)
 
     older = row > lane
+    older_low = older.astype(jnp.float32).astype(jnp.bfloat16)
+    newer_low = 1.0 - older_low
     length = length_ref[0]
     unseen = jnp.where(has_prev, 0.0, MASKED)
 
     def work(head):
+        for source in range(GROUP):
+            here = qg.at[head, :, pl.ds(source * TOK, TOK)]
+            pltpu.make_async_copy(here, here, qg_recv.at[head, source]).wait()
+
         @pl.when(has_prev)
         def _():
             for source in range(GROUP):
@@ -264,8 +273,6 @@
             first = part * TOK
             span = WINDOW + TOK
             seen = pl.ds(first, span)
-            here = qg.at[head, :, pl.ds(first, TOK)]
-            pltpu.make_async_copy(here, here, qg_recv.at[head, part]).wait()
             queries = qg[head, 0, first : first + TOK, :]
             grads = qg[head, 1, first : first + TOK, :]
             keys = kv[head, 0, seen, :]
@@ -309,9 +316,13 @@
                     axis=0,
                 )
 
+            def low_spread(merged):
+                top = merged[0:TOK]
+                return jnp.concatenate([top * older_low, merged[TOK:WINDOW], top * newer_low], axis=0)
+
             grad_full = spread(grad)
-            grad_low = grad_full.astype(jnp.bfloat16)
-            weight_full = spread(weight_low.astype(jnp.float32)).astype(jnp.bfloat16)
+            grad_low = low_spread(grad.astype(jnp.bfloat16))
+            weight_full = low_spread(weight_low)
             query_grad = dot(grad_low, keys, TN) * SCALE
             out_buf[head, 0, first : first + TOK, :] = query_grad.astype(jnp.bfloat16)
             key_part = dot(grad_low, queries, NN)
@@ -323,20 +334,21 @@
                     store[first : first + WINDOW, :] += fresh[0:WINDOW]
                     store[first + WINDOW : first + span, :] = fresh[WINDOW:span]
 
-        own_acc[head, 0] = key_acc[0, WINDOW:] * SCALE
-        own_acc[head, 1] = key_acc[1, WINDOW:]
-
 
         sums = col_acc[...]
         high = sums.astype(jnp.bfloat16)
         low = (sums - high.astype(jnp.float32)).astype(jnp.bfloat16)
-        by_query = dot(high, onehot[...], TN) + dot(low, onehot[...], TN)
-        bias_part[head] = jnp.sum(by_query, axis=0, keepdims=True)
+        by_query = dot(field_of_key[...], high, NN) + dot(field_of_key[...], low, NN)
+        bias_part[head] = jnp.sum(by_query.T, axis=0, keepdims=True)
 
     def give_back(head):
         ret_src[head, 0] = (key_acc[0, 0:WINDOW] * SCALE).astype(jnp.bfloat16)
         ret_src[head, 1] = key_acc[1, 0:WINDOW].astype(jnp.bfloat16)
 
+        own_acc[head, 0] = key_acc[0, WINDOW:] * SCALE
+        own_acc[head, 1] = key_acc[1, WINDOW:]
+
+    def send_back(head):
         @pl.when(has_prev)
         def _():
             pltpu.make_async_remote_copy(
@@ -405,6 +417,12 @@
                 hear(turn)
                 tell(turn + 1)
 
+        @pl.when(head == LOCAL_HEADS - 1)
+        def _():
+            for ready in range(LOCAL_HEADS - 1):
+                give_query(ready)
+            finish(0)
+
         work(head)
 
         @pl.when(head == 0)
@@ -433,6 +451,11 @@
 
         give_back(head)
 
+        @pl.when(head < LOCAL_HEADS - 2)
+        def _():
+            send_back(head)
+
+
     def rest_of(parts):
         return parts.at[pl.ds(0, parts.shape[0] - 1)]
 
@@ -445,8 +468,10 @@
             total = total + parts[index]
         return total
 
-    for head in range(LOCAL_HEADS):
-        give_query(head)
+    send_back(LOCAL_HEADS - 2)
+    send_back(LOCAL_HEADS - 1)
+    give_query(LOCAL_HEADS - 1)
+    for head in range(1, LOCAL_HEADS):
         finish(head)
 
     landed(plane_parts, plane_recv)
@@ -555,6 +580,7 @@
             pltpu.VMEM((heads, 2, WINDOW, HEAD_DIM), low_type),
             pltpu.VMEM((2 * GROUP, 1, TOK), jnp.int32),
             pltpu.VMEM((2 * WINDOW, 2 * FIELDS), low_type),
+            pltpu.VMEM((2 * FIELDS, 2 * WINDOW), low_type),
             pltpu.VMEM((2, 2 * WINDOW, HEAD_DIM), full_type),
             pltpu.VMEM((heads, 2, WINDOW, HEAD_DIM), full_type),
             pltpu.VMEM((2 * WINDOW, HEAD_DIM), full_type),

time: 64.1 us -> 59.9 us (0.934)
  Pallas kernels: 62.1 us -> 58.4 us
    pallas_call x1, Pallas kernels: 60.9 us -> 57.3 us  [shards(): pl.pallas_call(functools.partial(kernel, planes, copies), out_shape=(pltp...]
where the time goes in v4:
time: 59.9 us; the launch traced here: 59.7 us
  Pallas kernels  58.4 us (97%)
  between operations  1.29 us (2%)
    pallas_call x1, Pallas kernels, shards(): pl.pallas_call(functools.partial(kernel, planes, copies), out_shape=(pltp...  57.3 us

profile of v4, /device:TPU:1, one launch (start us, length us, event | category | flops | bytes accessed | tf_op | source)
XLA Modules:
  0.0 59.7 jit_solution(4489966962977672254)
XLA Ops:
  1.3 57.3 %shard_map.102 = (bf16[128,2048]{1,0:T(8,128)(2,1)S(1)}, bf16[128,2048]{1,0:T(8,128)(2,1)S(1)}, bf16[128,2048]{1,0:T(8,128)(2,1)S(1)}, f32[16,64]{1,0:T(8,128)S(1)}) custom-call(s32[1]{0:T(128)S(6)} %copy.11.length_ref, bf16[16,64]{1,0:T(8,128)(2,1)} %bias_ref.1, s32[1,128]{1,0:T(1,128)} %fields_ref.1, bf16[128,2048]{1,0:T(8,128)(2,1)} %bitcast.7, ...), custom_call_target="tpu_custom_call" | custom-call | tf_op jit(solution)/shard_map/pallas_call | solution.py:555
  58.5 1.2 %shard_map.103 = (bf16[128,2048]{1,0:T(8,128)(2,1)}, bf16[128,2048]{1,0:T(8,128)(2,1)}, bf16[128,2048]{1,0:T(8,128)(2,1)}, f32[16,64]{1,0:T(8,128)}) custom-call(bf16[128,2048]{1,0:T(8,128)(2,1)S(1)} %get-tuple-element.12.refs_0_, bf16[128,2048]{1,0:T(8,128)(2,1)S(1)} %get-tuple-element.13.refs_1_, bf16[128,2048]{1,0:T(8,128)(2,1)S(1)} %get-tuple-element.14.refs_2_, ...), custom_call_target="tpu_custom_call" | custom-call | tf_op jit(solution)/shard_map/pallas_call | solution.py:617

commit v5 on v4

--- a/solution.py
+++ b/solution.py
@@ -417,11 +417,10 @@
                 hear(turn)
                 tell(turn + 1)
 
-        @pl.when(head == LOCAL_HEADS - 1)
-        def _():
-            for ready in range(LOCAL_HEADS - 1):
+        @pl.when(head == LOCAL_HEADS - 2)
+        def _():
+            for ready in range(LOCAL_HEADS - 2):
                 give_query(ready)
-            finish(0)
 
         work(head)
 
@@ -470,16 +469,18 @@
 
     send_back(LOCAL_HEADS - 2)
     send_back(LOCAL_HEADS - 1)
+    give_query(LOCAL_HEADS - 2)
     give_query(LOCAL_HEADS - 1)
-    for head in range(1, LOCAL_HEADS):
+    for head in range(LOCAL_HEADS):
         finish(head)
 
     landed(plane_parts, plane_recv)
     mate_parts[seat] = sum_of(plane_parts)
     pl.semaphore_wait(rows_ready, copies - 1)
 
-    @pl.loop(1, mates)
-    def _(step):
+    @pl.loop(0, mates - 1)
+    def _(turn):
+        step = 1 + lax.rem(turn + 2 * GROUP, mates - 1)
         other = lax.rem(seat + step, mates)
         part = mate_parts.at[seat]
         pltpu.make_async_remote_copy(

time: 59.9 us -> 59.7 us (level)
  no operation moved by 1% of the time
where the time goes in v5:
time: 59.7 us; the launch traced here: 59.5 us
  Pallas kernels  58.2 us (97%)
  between operations  1.29 us (2%)
    pallas_call x1, Pallas kernels, shards(): pl.pallas_call(functools.partial(kernel, planes, copies), out_shape=(pltp...  57 us

profile of v5, /device:TPU:1, one launch (start us, length us, event | category | flops | bytes accessed | tf_op | source)
XLA Modules:
  0.0 59.5 jit_solution(1574901978423393779)
XLA Ops:
  1.3 57.0 %shard_map.102 = (bf16[128,2048]{1,0:T(8,128)(2,1)S(1)}, bf16[128,2048]{1,0:T(8,128)(2,1)S(1)}, bf16[128,2048]{1,0:T(8,128)(2,1)S(1)}, f32[16,64]{1,0:T(8,128)S(1)}) custom-call(s32[1]{0:T(128)S(6)} %copy.11.length_ref, bf16[16,64]{1,0:T(8,128)(2,1)} %bias_ref.1, s32[1,128]{1,0:T(1,128)} %fields_ref.1, bf16[128,2048]{1,0:T(8,128)(2,1)} %bitcast.7, ...), custom_call_target="tpu_custom_call" | custom-call | tf_op jit(solution)/shard_map/pallas_call | solution.py:556
  58.3 1.2 %shard_map.103 = (bf16[128,2048]{1,0:T(8,128)(2,1)}, bf16[128,2048]{1,0:T(8,128)(2,1)}, bf16[128,2048]{1,0:T(8,128)(2,1)}, f32[16,64]{1,0:T(8,128)}) custom-call(bf16[128,2048]{1,0:T(8,128)(2,1)S(1)} %get-tuple-element.12.refs_0_, bf16[128,2048]{1,0:T(8,128)(2,1)S(1)} %get-tuple-element.13.refs_1_, bf16[128,2048]{1,0:T(8,128)(2,1)S(1)} %get-tuple-element.14.refs_2_, ...), custom_call_target="tpu_custom_call" | custom-call | tf_op jit(solution)/shard_map/pallas_call | solution.py:618

commit v6 on v5

--- a/solution.py
+++ b/solution.py
@@ -14,6 +14,7 @@
 TOK = 128
 GROUP = WINDOW // TOK
 LOCAL_HEADS = HEADS // GROUP
+PIECES = 4
 SCALE = HEAD_DIM**-0.5
 LOG2E = 1.4426950408889634
 MASKED = -1e30
@@ -536,9 +537,17 @@
 def copy_kernel(*refs):
     count = len(refs) // 2
     sources, targets, sems = refs[:count], refs[count : 2 * count], refs[-1]
-    moves = [
-        pltpu.make_async_copy(sources[index], targets[index], sems.at[index]) for index in range(count)
-    ]
+    moves = []
+    for index in range(count):
+        rows = sources[index].shape[0]
+        piece = max(rows // PIECES, 16)
+        for turn, first in enumerate(range(0, rows, piece)):
+            part = pl.ds(first, piece)
+            moves.append(
+                pltpu.make_async_copy(
+                    sources[index].at[part], targets[index].at[part], sems.at[index, turn]
+                )
+            )
     for move in moves:
         move.start()
     for move in moves:
@@ -620,7 +629,7 @@
         out_shape=tuple(jax.ShapeDtypeStruct(one.shape, one.dtype) for one in results),
         in_specs=[in_vmem] * 4,
         out_specs=(in_hbm,) * 4,
-        scratch_shapes=[dma((4,))],
+        scratch_shapes=[dma((4, PIECES))],
         compiler_params=pltpu.CompilerParams(vmem_limit_bytes=2**20),
     )(*results)
     return query_grad[None], key_grad[None], value_grad[None], bias_total

time: 59.7 us -> 59.8 us (level)
  no operation moved by 1% of the time
where the time goes in v6:
time: 59.8 us; the launch traced here: 59.6 us
  Pallas kernels  58.3 us (97%)
  between operations  1.29 us (2%)
    pallas_call x1, Pallas kernels, shards(): pl.pallas_call(functools.partial(kernel, planes, copies), out_shape=(pltp...  57 us
    pallas_call x1, Pallas kernels, shards(): pl.pallas_call(copy_kernel, out_shape=tuple((jax.ShapeDtypeStruct(one.sha...  1.27 us

profile of v6, /device:TPU:1, one launch (start us, length us, event | category | flops | bytes accessed | tf_op | source)
XLA Modules:
  0.0 59.6 jit_solution(11925677391204813937)
XLA Ops:
  1.3 57.0 %shard_map.102 = (bf16[128,2048]{1,0:T(8,128)(2,1)S(1)}, bf16[128,2048]{1,0:T(8,128)(2,1)S(1)}, bf16[128,2048]{1,0:T(8,128)(2,1)S(1)}, f32[16,64]{1,0:T(8,128)S(1)}) custom-call(s32[1]{0:T(128)S(6)} %copy.11.length_ref, bf16[16,64]{1,0:T(8,128)(2,1)} %bias_ref.1, s32[1,128]{1,0:T(1,128)} %fields_ref.1, bf16[128,2048]{1,0:T(8,128)(2,1)} %bitcast.7, ...), custom_call_target="tpu_custom_call" | custom-call | tf_op jit(solution)/shard_map/pallas_call | solution.py:565
  58.3 1.3 %shard_map.103 = (bf16[128,2048]{1,0:T(8,128)(2,1)}, bf16[128,2048]{1,0:T(8,128)(2,1)}, bf16[128,2048]{1,0:T(8,128)(2,1)}, f32[16,64]{1,0:T(8,128)}) custom-call(bf16[128,2048]{1,0:T(8,128)(2,1)S(1)} %get-tuple-element.12.refs_0_, bf16[128,2048]{1,0:T(8,128)(2,1)S(1)} %get-tuple-element.13.refs_1_, bf16[128,2048]{1,0:T(8,128)(2,1)S(1)} %get-tuple-element.14.refs_2_, ...), custom_call_target="tpu_custom_call" | custom-call | tf_op jit(solution)/shard_map/pallas_call | solution.py:627
